TPU v7x, 32 devices: a whole 2x2x4 slice. The times are simulated.
32 devices in a mesh: dp: 4 (over y, x), expert: 8 (over z, core).
Axes of the slice: x: 2, y: 2, z: 4, core: 2. Of those that a mesh axis runs over, the one named last changes fastest.
Arguments:
- layer_input: bfloat16 [6144, 2048], P(('dp', 'expert')), may hold values from -6 to 6
- out_cotangent: bfloat16 [6144, 2048], P(('dp', 'expert')), may hold values from -6 to 6
- segments: int32 [32, 192], P(('dp', 'expert')), may hold values from 0 to 2, never falling along the last dimension, each value on 1 to 96 neighbouring positions
- routes: int32 [6144, 8], P(('dp', 'expert')), may hold values from 0 to 23, all different within a row; in each aligned block of 192 rows (0 to 191, 192 to 383, ...) at most 72 rows name the same one
- w_qkv: bfloat16 [2048, 6144], P(('dp', 'expert')), may hold values from -0.125 to 0.125
- w_out: bfloat16 [2048, 2048], P(('dp', 'expert')), may hold values from -0.5 to 0.5
- w_router: bfloat16 [2048, 24], P(('dp', 'expert')), may hold values from -0.0625 to 0.0625
- attn_gain: bfloat16 [2048], P(('dp', 'expert')), may hold values from 0.5 to 1.5
- mlp_gain: bfloat16 [2048], P(('dp', 'expert')), may hold values from 0.5 to 1.5
- query_gain: bfloat16 [2048], P(('dp', 'expert')), may hold values from 0.099609375 to 1.8984375
- key_gain: bfloat16 [2048], P(('dp', 'expert')), may hold values from 0.099609375 to 1.8984375
- w_gate_up: bfloat16 [24, 2048, 2048], P('expert'), may hold values from -0.125 to 0.125
- w_down: bfloat16 [24, 1024, 2048], P('expert'), may hold values from -0.75 to 0.75
Outputs:
- out: bfloat16 [6144, 2048], P(('dp', 'expert'))
- grad_input: float32 [6144, 2048], P(('dp', 'expert'))
- grad_qkv: float32 [2048, 3, 2048], P('dp', None, 'expert')
- grad_out: float32 [2048, 2048], P('expert', 'dp')
- grad_router: float32 [2048, 24], P(('dp', 'expert'))
- grad_attn_gain: float32 [2048], P(('dp', 'expert'))
- grad_mlp_gain: float32 [2048], P(('dp', 'expert'))
- grad_query_gain: float32 [2048], P('expert')
- grad_key_gain: float32 [2048], P('expert')
- grad_gate_up: float32 [24, 2048, 2048], P('expert', 'dp')
- grad_down: float32 [24, 1024, 2048], P('expert', 'dp')
Inputs may be any that keep to these rules, and one draw needn't show every extreme that they name: `routes`: each row names 8 different experts. Among the rows of one device no expert is named more than 72 times, a bound that some block reaches. `segments`: within a sequence the numbers never fall; a document has at most 96 tokens and one has exactly that many.
All inputs are finite; a program needn't handle non-finite values.
Results may differ from a plain program's by a relative error of at most 0.02.
Values may be sent and summed in bfloat16 or wider, within the bound.
A program may use at most 320 MiB of HBM per device.

v0:
```python
import math
import jax
import jax.numpy as jnp
from jax import lax
from jax.sharding import PartitionSpec as P

HEADS = 16
NORM_EPS = 1e-05


def rms_scale(values):
    return lax.rsqrt(jnp.mean(values * values, axis=-1, keepdims=True) + NORM_EPS)


def rotary(values, direction):
    length = values.shape[-3]
    half_size = values.shape[-1] // 2
    index_half = jnp.arange(half_size, dtype=jnp.float32)
    frequency = jnp.exp(index_half * (-2.0 * math.log(10000.0) / values.shape[-1]))
    angles = jnp.arange(length, dtype=jnp.float32)[:, None] * frequency[None, :]
    cosine = jnp.cos(angles)[:, None, :]
    sine_table = direction * jnp.sin(angles)[:, None, :]
    first_half = values[..., :half_size]
    second = values[..., half_size:]
    return jnp.concatenate(
        [first_half * cosine - second * sine_table, second * cosine + first_half * sine_table],
        axis=-1,
    )


def norm_back(grad_normed, normed, scale_rows):
    return scale_rows * (
        grad_normed - normed * jnp.mean(grad_normed * normed, axis=-1, keepdims=True)
    )


def contract_rows(left_side, right_side):
    return lax.dot_general(
        left_side, right_side, (((0,), (0,)), ((), ())), preferred_element_type=jnp.float32
    )


def contract_cols(left_side, right_side):
    return lax.dot_general(
        left_side, right_side, (((1,), (1,)), ((), ())), preferred_element_type=jnp.float32
    )


def masked_scores(query_rot, key_rot, allowed, scaling):
    raw_scores = (
        jnp.einsum("gqhd,gkhd->ghqk", query_rot, key_rot, preferred_element_type=jnp.float32)
        * scaling
    )
    return jnp.where(allowed[:, None], raw_scores, -1e30)


def on_device(
    layer_input,
    out_cotangent,
    segments,
    routes,
    w_qkv,
    w_out,
    w_router,
    attn_gain,
    mlp_gain,
    query_gain,
    key_gain,
    w_gate_up,
    w_down,
):
    row_count, model_dim = layer_input.shape
    top_count = routes.shape[1]
    expert_count = w_router.shape[1]
    head_size = model_dim // HEADS
    capacity = (row_count * top_count * 9 // 8 + expert_count - 1) // expert_count
    slot_count = expert_count * capacity
    scaling = 1.0 / math.sqrt(head_size)
    dp_count = lax.axis_size("dp")
    dense = (w_qkv, w_out, w_router, attn_gain, mlp_gain, query_gain, key_gain)
    qkv_full, out_full, router_full, gain_attn, gain_mlp, gain_query, gain_key = (
        lax.all_gather(dense[0], ("dp", "expert"), axis=0, tiled=True),
        lax.all_gather(dense[1], ("dp", "expert"), axis=0, tiled=True),
        lax.all_gather(dense[2], ("dp", "expert"), axis=0, tiled=True),
        lax.all_gather(dense[3], ("dp", "expert"), axis=0, tiled=True),
        lax.all_gather(dense[4], ("dp", "expert"), axis=0, tiled=True),
        lax.all_gather(dense[5], ("dp", "expert"), axis=0, tiled=True),
        lax.all_gather(dense[6], ("dp", "expert"), axis=0, tiled=True),
    )
    gain_attn = gain_attn.astype(jnp.float32)
    gain_mlp = gain_mlp.astype(jnp.float32)
    gain_query = gain_query.astype(jnp.float32)
    gain_key = gain_key.astype(jnp.float32)
    inputs = layer_input.astype(jnp.float32)
    scale_attn = rms_scale(inputs)
    normed_attn = inputs * scale_attn
    hidden_one = (normed_attn * gain_attn).astype(jnp.bfloat16)
    group_count = segments.shape[0]
    heads_here = model_dim // head_size
    projected = jnp.dot(hidden_one, qkv_full, preferred_element_type=jnp.float32)
    query_rows = projected[:, :model_dim]
    key_rows = projected[:, model_dim : 2 * model_dim]
    value_rows = projected[:, 2 * model_dim :]
    square_query = jnp.sum(query_rows * query_rows, axis=-1, keepdims=True)
    square_key = jnp.sum(key_rows * key_rows, axis=-1, keepdims=True)
    scale_query = lax.rsqrt(square_query / model_dim + NORM_EPS)
    scale_key = lax.rsqrt(square_key / model_dim + NORM_EPS)
    normed_query = query_rows * scale_query
    normed_key = key_rows * scale_key
    head_shape = (group_count, row_count, heads_here, head_size)
    query_rot = rotary((normed_query * gain_query).reshape(head_shape), 1.0).astype(jnp.bfloat16)
    key_rot = rotary((normed_key * gain_key).reshape(head_shape), 1.0).astype(jnp.bfloat16)
    value_low = value_rows.reshape(head_shape).astype(jnp.bfloat16)
    position = jnp.arange(row_count)
    allowed = (position[:, None] >= position[None, :])[None] & (
        segments[:, :, None] == segments[:, None, :]
    )
    scores = masked_scores(query_rot, key_rot, allowed, scaling)
    row_top = jnp.max(scores, axis=-1, keepdims=True)
    expanded = jnp.exp(scores - row_top)
    row_total = jnp.sum(expanded, axis=-1, keepdims=True)
    log_total = row_top + jnp.log(row_total)
    attn_low = (expanded / row_total).astype(jnp.bfloat16)
    attended = jnp.einsum(
        "ghqk,gkhd->gqhd", attn_low, value_low, preferred_element_type=jnp.float32
    )
    attended = attended.reshape(group_count * row_count, model_dim).astype(jnp.bfloat16)
    attn_proj = jnp.dot(attended, out_full, preferred_element_type=jnp.float32)
    residual = inputs + attn_proj
    scale_mlp = rms_scale(residual)
    normed_mlp = residual * scale_mlp
    hidden_two = (normed_mlp * gain_mlp).astype(jnp.bfloat16)
    logits = jnp.dot(hidden_two, router_full, preferred_element_type=jnp.float32)
    chooser = (routes[:, :, None] == jnp.arange(expert_count)[None, None, :]).astype(jnp.float32)
    chosen = jnp.sum(chooser * logits[:, None, :], axis=-1)
    gate_values = jax.nn.softmax(chosen, axis=-1)
    used_table = jnp.sum(chooser, axis=1).astype(jnp.bfloat16)
    lower_tri = (position[:, None] > position[None, :]).astype(jnp.bfloat16)
    earlier = jnp.dot(lower_tri, used_table, preferred_element_type=jnp.float32)
    rank_in = jnp.sum(chooser * earlier[:, None, :], axis=-1).astype(jnp.int32)
    slot_index = routes * capacity + rank_in
    slot_flat = slot_index.reshape(-1)
    dispatch_table = jnp.any(
        slot_index[None, :, :] == jnp.arange(slot_count)[:, None, None], axis=-1
    ).astype(jnp.bfloat16)
    send_rows = jnp.dot(dispatch_table, hidden_two, preferred_element_type=jnp.float32).astype(
        jnp.bfloat16
    )
    send_rows = send_rows.reshape(expert_count, capacity, model_dim)
    expert_rows = lax.all_to_all(send_rows, "expert", split_axis=0, concat_axis=1, tiled=True)
    hidden = jnp.einsum("erd,edf->erf", expert_rows, w_gate_up, preferred_element_type=jnp.float32)
    hidden_size = hidden.shape[2] // 2
    gate_part = hidden[..., :hidden_size]
    up_part = hidden[..., hidden_size:]
    sigmoid_gate = jax.nn.sigmoid(gate_part)
    silu_gate = gate_part * sigmoid_gate
    activated = (silu_gate * up_part).astype(jnp.bfloat16)
    expert_out = jnp.einsum(
        "erf,efd->erd", activated, w_down, preferred_element_type=jnp.float32
    ).astype(jnp.bfloat16)
    returned = lax.all_to_all(
        expert_out, "expert", split_axis=1, concat_axis=0, tiled=True
    ).reshape(slot_count, model_dim)
    picked = (
        jnp.take(returned, slot_flat, axis=0)
        .reshape(row_count, top_count, model_dim)
        .astype(jnp.float32)
    )
    mixture = jnp.sum(gate_values[:, :, None] * picked, axis=1)
    output = (residual + mixture).astype(jnp.bfloat16)
    grad_out_rows = out_cotangent.astype(jnp.float32)
    grad_gates = jnp.sum(picked * grad_out_rows[:, None, :], axis=-1)
    grad_slots = (
        (gate_values[:, :, None] * grad_out_rows[:, None, :])
        .astype(jnp.bfloat16)
        .reshape(row_count * top_count, model_dim)
    )
    back_send = jnp.zeros((slot_count, model_dim), jnp.bfloat16).at[slot_flat].set(grad_slots)
    back_send = back_send.reshape(expert_count, capacity, model_dim)
    grad_expert_out = lax.all_to_all(back_send, "expert", split_axis=0, concat_axis=1, tiled=True)
    grad_act = jnp.einsum(
        "erd,efd->erf", grad_expert_out, w_down, preferred_element_type=jnp.float32
    )
    grad_w_down = jnp.einsum(
        "erf,erd->efd", activated, grad_expert_out, preferred_element_type=jnp.float32
    )
    grad_gate = grad_act * up_part * sigmoid_gate * (1.0 + gate_part * (1.0 - sigmoid_gate))
    grad_up = grad_act * silu_gate
    grad_hidden = jnp.concatenate([grad_gate, grad_up], axis=-1).astype(jnp.bfloat16)
    grad_w_gate_up = jnp.einsum(
        "erd,erf->edf", expert_rows, grad_hidden, preferred_element_type=jnp.float32
    )
    grad_rows = jnp.einsum(
        "erf,edf->erd", grad_hidden, w_gate_up, preferred_element_type=jnp.float32
    ).astype(jnp.bfloat16)
    grad_back = lax.all_to_all(
        grad_rows, "expert", split_axis=1, concat_axis=0, tiled=True
    ).reshape(slot_count, model_dim)
    grad_two = contract_rows(dispatch_table, grad_back)
    grad_chosen = gate_values * (
        grad_gates - jnp.sum(gate_values * grad_gates, axis=-1, keepdims=True)
    )
    grad_logits = jnp.sum(chooser * grad_chosen[:, :, None], axis=1).astype(jnp.bfloat16)
    grad_router = contract_rows(hidden_two, grad_logits)
    grad_two = grad_two + contract_cols(grad_logits, router_full)
    grad_gain_mlp = jnp.sum(grad_two * normed_mlp, axis=0)
    grad_resid = grad_out_rows + norm_back(grad_two * gain_mlp, normed_mlp, scale_mlp)
    grad_attn = grad_resid.astype(jnp.bfloat16)
    grad_w_out = contract_rows(attended, grad_attn)
    grad_attended = contract_cols(grad_attn, out_full).astype(jnp.bfloat16).reshape(head_shape)
    attn_again = jnp.exp(masked_scores(query_rot, key_rot, allowed, scaling) - log_total)
    attn_again_low = attn_again.astype(jnp.bfloat16)
    grad_value = jnp.einsum(
        "ghqk,gqhd->gkhd", attn_again_low, grad_attended, preferred_element_type=jnp.float32
    )
    grad_attn_weights = jnp.einsum(
        "gqhd,gkhd->ghqk", grad_attended, value_low, preferred_element_type=jnp.float32
    )
    row_delta = jnp.sum(grad_attn_weights * attn_again, axis=-1, keepdims=True)
    grad_scores = (attn_again * (grad_attn_weights - row_delta)).astype(jnp.bfloat16)
    grad_query_rot = (
        jnp.einsum("ghqk,gkhd->gqhd", grad_scores, key_rot, preferred_element_type=jnp.float32)
        * scaling
    )
    grad_key_rot = (
        jnp.einsum("ghqk,gqhd->gkhd", grad_scores, query_rot, preferred_element_type=jnp.float32)
        * scaling
    )
    grad_query_normed = rotary(grad_query_rot, -1.0).reshape(group_count * row_count, model_dim)
    grad_key_normed = rotary(grad_key_rot, -1.0).reshape(group_count * row_count, model_dim)
    grad_gain_query = jnp.sum(grad_query_normed * normed_query, axis=0)
    grad_gain_key = jnp.sum(grad_key_normed * normed_key, axis=0)
    weighted_query = grad_query_normed * gain_query
    weighted_key = grad_key_normed * gain_key
    dot_query = jnp.sum(weighted_query * normed_query, axis=-1, keepdims=True)
    dot_key = jnp.sum(weighted_key * normed_key, axis=-1, keepdims=True)
    grad_query = scale_query * (weighted_query - normed_query * (dot_query / model_dim))
    grad_key = scale_key * (weighted_key - normed_key * (dot_key / model_dim))
    grad_proj = jnp.concatenate(
        [grad_query, grad_key, grad_value.reshape(group_count * row_count, model_dim)], axis=-1
    ).astype(jnp.bfloat16)
    grad_w_qkv = contract_rows(hidden_one, grad_proj).reshape(model_dim, 3, model_dim)
    grad_one = contract_cols(grad_proj, qkv_full)
    grad_gain_attn = jnp.sum(grad_one * normed_attn, axis=0)
    grad_inputs = grad_resid + norm_back(grad_one * gain_attn, normed_attn, scale_attn)
    gain_pair = jnp.stack([grad_gain_query, grad_gain_key])
    head_qkv, head_out, head_gains = (
        lax.psum_scatter(
            grad_w_qkv.astype(jnp.bfloat16), "expert", scatter_dimension=2, tiled=True
        ).astype(jnp.float32),
        lax.psum_scatter(
            grad_w_out.astype(jnp.bfloat16), "expert", scatter_dimension=0, tiled=True
        ).astype(jnp.float32),
        lax.psum_scatter(
            gain_pair.astype(jnp.bfloat16), "expert", scatter_dimension=1, tiled=True
        ).astype(jnp.float32),
    )
    spread_gains = jnp.broadcast_to(head_gains[None], (dp_count,) + head_gains.shape)
    summed = (
        lax.psum_scatter(
            head_qkv.astype(jnp.bfloat16), "dp", scatter_dimension=0, tiled=True
        ).astype(jnp.float32),
        lax.psum_scatter(
            head_out.astype(jnp.bfloat16), "dp", scatter_dimension=1, tiled=True
        ).astype(jnp.float32),
        lax.psum_scatter(
            spread_gains.astype(jnp.bfloat16), "dp", scatter_dimension=0, tiled=True
        ).astype(jnp.float32),
        lax.psum_scatter(
            grad_w_gate_up.astype(jnp.bfloat16), "dp", scatter_dimension=1, tiled=True
        ).astype(jnp.float32),
        lax.psum_scatter(
            grad_w_down.astype(jnp.bfloat16), "dp", scatter_dimension=1, tiled=True
        ).astype(jnp.float32),
    )
    shared = (
        lax.psum_scatter(grad_router, ("dp", "expert"), scatter_dimension=0, tiled=True),
        lax.psum_scatter(grad_gain_attn, ("dp", "expert"), scatter_dimension=0, tiled=True),
        lax.psum_scatter(grad_gain_mlp, ("dp", "expert"), scatter_dimension=0, tiled=True),
    )
    return (
        output,
        grad_inputs,
        summed[0],
        summed[1],
        shared[0],
        shared[1],
        shared[2],
        summed[2][0, 0],
        summed[2][0, 1],
        summed[3],
        summed[4],
    )


def solution(mesh):
    placed = (
        P(("dp", "expert"), None),
        P(("dp", "expert"), None),
        P(("dp", "expert"), None),
        P(("dp", "expert"), None),
        P(("dp", "expert"), None),
        P(("dp", "expert"), None),
        P(("dp", "expert"), None),
        P(("dp", "expert")),
        P(("dp", "expert")),
        P(("dp", "expert")),
        P(("dp", "expert")),
        P("expert", None, None),
        P("expert", None, None),
    )
    return jax.shard_map(
        on_device,
        mesh=mesh,
        in_specs=placed,
        out_specs=(
            P(("dp", "expert"), None),
            P(("dp", "expert"), None),
            P("dp", None, "expert"),
            P("expert", "dp"),
            P(("dp", "expert"), None),
            P(("dp", "expert")),
            P(("dp", "expert")),
            P("expert"),
            P("expert"),
            P("expert", "dp", None),
            P("expert", "dp", None),
        ),
        check_vma=False,
    )
```

profile of v0, /device:TPU:0, one launch (start us, length us, event | category | flops | bytes accessed | tf_op | source)
XLA Modules:
  0.0 2162.2 jit_solution(9898101751853634901)
XLA Ops:
  12.1 43.5 %all-reduce.8 = (bf16[2048]{0:T(1024)(128)(2,1)S(1)}, bf16[2048]{0:T(1024)(128)(2,1)S(1)}, bf16[2048]{0:T(1024)(128)(2,1)S(1)}, bf16[2048]{0:T(1024)(128)(2,1)S(1)}) all-reduce(bf16[2048]{0:T(1024)(128)(2,1)S(1)} %dynamic-update-slice, bf16[2048]{0:T(1024)(128)(2,1)S(1)} %dynamic-update-slice.2, ...), channel_id=1, replica_groups=mesh['dp'=4,'expert'=8] {'dp','expert'}, use_global_device_ids=true, to_apply=%add | all-reduce | flops 8192 | bytes 32768
  55.7 41.7 %all-gather = bf16[32,64,24]{1,2,0:T(8,128)(2,1)S(1)} all-gather(bf16[1,64,24]{1,2,0:T(8,128)(2,1)} %bitcast.186), channel_id=1, replica_groups=mesh['dp'=4,'expert'=8] {'dp','expert'}, dimensions={0}, use_global_device_ids=true | all-gather | bytes 101376 | tf_op jit(solution)/shard_map/all_gather | solution.py:84
  100.0 71.0 %all-gather.4.cloned.1.call-done = bf16[2048,6144]{1,0:T(8,128)(2,1)} async-done(((bf16[64,6144]{1,0:T(8,128)(2,1)}), bf16[2048,6144]{1,0:T(8,128)(2,1)}) %all-gather.4.cloned.1.call-update) | async-done | bytes 25165840 | tf_op jit(solution)/shard_map/all_gather | solution.py:82
  191.8 57.7 %all-gather.6.cloned.1.call-done = bf16[2048,2048]{1,0:T(8,128)(2,1)} async-done(((bf16[64,2048]{1,0:T(8,128)(2,1)}), bf16[2048,2048]{1,0:T(8,128)(2,1)}) %all-gather.6.cloned.1.call-update) | async-done | bytes 8388624 | tf_op jit(solution)/shard_map/all_gather | solution.py:83
  256.8 19.1 fusion.2
  278.0 159.0 %all_to_all.66 = bf16[24,72,2048]{2,1,0:T(8,128)(2,1)S(1)} all-to-all(bf16[24,72,2048]{2,1,0:T(8,128)(2,1)S(1)} %bitcast.163), channel_id=1, replica_groups=mesh['dp'=4,'expert'=8] {'expert'}, dimensions={0} | all-to-all | bytes 14155776 | tf_op jit(solution)/shard_map/all_to_all | solution.py:150
  440.6 24.6 %fusion.85 = f32[3,576,2048]{2,1,0:T(8,128)} fusion(bf16[3,576,2048]{2,1,0:T(8,128)(2,1)} %bitcast.160, bf16[3,2048,2048]{2,1,0:T(8,128)(2,1)} %param.24), kind=kOutput, calls=%fused_computation.172 | convolution fusion | flops 14495514624 | bytes 46399488 | tf_op jit(solution)/shard_map/erd,edf->erf/dot_general | solution.py:151
  485.5 22.9 %copy.145 = bf16[3,576,2048]{2,0,1:T(4,128)(2,1)} copy(bf16[3,576,2048]{2,1,0:T(8,128)(2,1)S(1)} %convolution_convert_fusion.6) | data formatting | bytes 14155776 | tf_op jit(solution)/shard_map/convert_element_type | solution.py:160
  514.7 205.7 %all-to-all-done.1 = bf16[3,576,2048]{2,0,1:T(4,128)(2,1)} async-done(((bf16[3,576,2048]{2,0,1:T(4,128)(2,1)}), bf16[3,576,2048]{2,0,1:T(4,128)(2,1)}, u32[]{:S(2)}, u32[]{:S(2)}) %all-to-all-start.1) | async-done | bytes 7077920 | tf_op jit(solution)/shard_map/all_to_all | solution.py:161
  732.2 16.6 gather_fusion
  768.3 159.7 %all_to_all.67 = bf16[24,72,2048]{2,1,0:T(8,128)(2,1)S(1)} all-to-all(bf16[24,72,2048]{2,1,0:T(8,128)(2,1)} %bitcast.166), channel_id=1, replica_groups=mesh['dp'=4,'expert'=8] {'expert'}, dimensions={0} | all-to-all | bytes 14155776 | tf_op jit(solution)/shard_map/all_to_all | solution.py:180
  931.8 22.4 %multiply_convert_fusion.1 = (bf16[3,576,1024]{2,1,0:T(8,128)(2,1)}, bf16[3,576,1024]{2,1,0:T(8,128)(2,1)}) fusion(f32[3,576,2048]{2,1,0:T(8,128)} %fusion.85, bf16[3,576,2048]{2,1,0:T(8,128)(2,1)} %bitcast.176, bf16[3,1024,2048]{2,1,0:T(8,128)(2,1)} %param.25), kind=kOutput, calls=%fused_computation.15 | convolution fusion | flops 7270760448 | bytes 40894464 | tf_op jit(solution)/shard_map/erd,efd->erf/dot_general | solution.py:181
  954.1 21.6 convolution_convert_fusion.5
  1001.5 197.3 %all-to-all-done.3 = bf16[3,576,2048]{2,0,1:T(4,128)(2,1)} async-done(((bf16[3,576,2048]{2,0,1:T(4,128)(2,1)}), bf16[3,576,2048]{2,0,1:T(4,128)(2,1)}, u32[]{:S(2)}, u32[]{:S(2)}) %all-to-all-start.3) | async-done | bytes 7077920 | tf_op jit(solution)/shard_map/all_to_all | solution.py:196
  1261.0 32.6 %copy.163 = bf16[2048,6144]{0,1:T(8,128)(2,1)} copy(bf16[2048,6144]{1,0:T(8,128)(2,1)} %convolution_convert_fusion) | data formatting | bytes 50331648 | tf_op jit(solution)/shard_map/convert_element_type | solution.py:249
  1297.5 16.6 convolution_convert_fusion.4
  1315.2 26.6 %convolution_convert_fusion.1 = bf16[3,2048,2048]{2,1,0:T(8,128)(2,1)} fusion(bf16[3,576,2048]{2,1,0:T(8,128)(2,1)} %bitcast.161, bf16[3,576,1024]{2,1,0:T(8,128)(2,1)} %get-tuple-element.80, bf16[3,576,1024]{2,1,0:T(8,128)(2,1)} %get-tuple-element.79), kind=kOutput, calls=%fused_computation.5 | convolution fusion | flops 14522253312 | bytes 39321600 | tf_op jit(solution)/shard_map/erd,erf->edf/dot_general | solution.py:190
  1341.9 218.4 %reduce-scatter.13.cloned.1.call-done = bf16[2048,3,256]{0,2,1:T(8,128)(2,1)} async-done(((bf16[2048,3,2048]{0,2,1:T(8,128)(2,1)}), bf16[2048,3,256]{0,2,1:T(8,128)(2,1)}) %reduce-scatter.13.cloned.1.call-update) | async-done | bytes 3145744 | tf_op jit(solution)/shard_map/reduce_scatter | solution.py:248
  1560.9 135.3 %reduce-scatter.25.cloned.1.call-done = f32[64,24]{1,0:T(8,128)} async-done(((f32[2048,24]{1,0:T(8,128)}), f32[64,24]{1,0:T(8,128)}) %reduce-scatter.25.cloned.1.call-update) | async-done | bytes 6160
  1712.5 37.2 %all-reduce.7 = (f32[2048]{0:T(1024)S(1)}, f32[2048]{0:T(1024)S(1)}) all-reduce(f32[2048]{0:T(1024)S(1)} %get-tuple-element.65, f32[2048]{0:T(1024)S(1)} %get-tuple-element.63), channel_id=7, replica_groups=mesh['dp'=4,'expert'=8] {'dp','expert'}, use_global_device_ids=true, to_apply=%region_28.29.clone | all-reduce | flops 4096 | bytes 32768
  1766.1 83.5 %reduce-scatter.23.cloned.1.call-done = bf16[3,256,2048]{2,1,0:T(8,128)(2,1)} async-done(((bf16[3,1024,2048]{2,1,0:T(8,128)(2,1)}), bf16[3,256,2048]{2,1,0:T(8,128)(2,1)}) %reduce-scatter.23.cloned.1.call-update) | async-done | bytes 3145744 | tf_op jit(solution)/shard_map/reduce_scatter | solution.py:272
  1855.0 25.2 %reduce-scatter.19.cloned.1.call-done = bf16[256,512]{1,0:T(8,128)(2,1)} async-done(((bf16[256,2048]{1,0:T(8,128)(2,1)}), bf16[256,512]{1,0:T(8,128)(2,1)}) %reduce-scatter.19.cloned.1.call-update) | async-done | bytes 262160 | tf_op jit(solution)/shard_map/reduce_scatter | solution.py:263
  1882.0 223.5 %reduce-scatter.21.cloned.1.call-done = bf16[3,512,2048]{2,1,0:T(8,128)(2,1)} async-done(((bf16[3,2048,2048]{2,1,0:T(8,128)(2,1)}), bf16[3,512,2048]{2,1,0:T(8,128)(2,1)}) %reduce-scatter.21.cloned.1.call-update) | async-done | bytes 6291472 | tf_op jit(solution)/shard_map/reduce_scatter | solution.py:269
  2114.6 37.7 %reduce-scatter.15.cloned.1.call-done = bf16[512,3,256]{0,2,1:T(8,128)(2,1)} async-done(((bf16[2048,3,256]{0,2,1:T(8,128)(2,1)}), bf16[512,3,256]{0,2,1:T(8,128)(2,1)}) %reduce-scatter.15.cloned.1.call-update) | async-done | bytes 786448 | tf_op jit(solution)/shard_map/reduce_scatter | solution.py:260
  (250 shorter events, 247.1 us)
Async XLA Ops:
  7.2 91.3 %copy-start.7 = (bf16[192,2048]{1,0:T(8,128)(2,1)S(1)}, bf16[192,2048]{1,0:T(8,128)(2,1)}, u32[]{:S(2)}) copy-start(bf16[192,2048]{1,0:T(8,128)(2,1)} %param.13) | copy-start | bytes 2359300
  7.2 91.7 %copy-start.52 = (s32[1,192]{1,0:T(1,128)S(1)}, s32[1,192]{1,0:T(1,128)}, u32[]{:S(2)}) copy-start(s32[1,192]{1,0:T(1,128)} %param.15) | copy-start | bytes 2308
  7.2 163.8 %all-gather.4.cloned.1.call-start = ((), (), s32[]{:S(2)}) async-start(), calls=%async_computation.12 | async-start | bytes 25952256 | tf_op jit(solution)/shard_map/all_gather | solution.py:82
  7.9 241.6 %all-gather.6.cloned.1.call-start = ((), (), s32[]{:S(2)}) async-start(), calls=%async_computation.13 | async-start | bytes 8650752 | tf_op jit(solution)/shard_map/all_gather | solution.py:83
  55.6 126.6 %copy-start.30 = (f32[2048]{0:T(1024)}, f32[2048]{0:T(1024)S(1)}, u32[]{:S(2)}) copy-start(f32[2048]{0:T(1024)S(1)} %convert_element_type.154) | copy-start | bytes 24580
  55.6 126.9 %copy-start.34 = (f32[2048]{0:T(1024)}, f32[2048]{0:T(1024)S(1)}, u32[]{:S(2)}) copy-start(f32[2048]{0:T(1024)S(1)} %convert_element_type.158) | copy-start | bytes 24580
  55.6 126.9 %copy-start.36 = (f32[2048]{0:T(1024)}, f32[2048]{0:T(1024)S(1)}, u32[]{:S(2)}) copy-start(f32[2048]{0:T(1024)S(1)} %convert_element_type.157) | copy-start | bytes 24580
  55.6 199.3 %copy-start.38 = (f32[2048]{0:T(1024)}, f32[2048]{0:T(1024)S(1)}, u32[]{:S(2)}) copy-start(f32[2048]{0:T(1024)S(1)} %convert_element_type.164) | copy-start | bytes 24580
  97.7 158.6 %copy-start.27 = (bf16[2048,24]{0,1:T(8,128)(2,1)}, bf16[2048,24]{0,1:T(8,128)(2,1)S(1)}, u32[]{:S(2)}) copy-start(bf16[2048,24]{0,1:T(8,128)(2,1)S(1)} %reshape.545) | copy-start | bytes 294916
  98.7 83.5 %copy-start.44 = (f32[192]{0:T(256)}, f32[192]{0:T(256)S(1)}, u32[]{:S(2)}) copy-start(f32[192]{0:T(256)S(1)} %add_rsqrt_fusion.3) | copy-start | bytes 2308
  100.0 84.9 %copy-start.25 = (f32[192,64]{1,0:T(8,128)}, f32[192,64]{1,0:T(8,128)S(1)}, u32[]{:S(2)}) copy-start(f32[192,64]{1,0:T(8,128)S(1)} %get-tuple-element.107) | copy-start | bytes 147460
  191.8 63.1 %copy-start.19 = (bf16[1,192,16,128]{3,2,1,0:T(8,128)(2,1)}, bf16[1,192,16,128]{3,2,1,0:T(8,128)(2,1)S(1)}, u32[]{:S(2)}) copy-start(bf16[1,192,16,128]{3,2,1,0:T(8,128)(2,1)S(1)} %copy.139) | copy-start | bytes 2359300
  508.4 212.0 %all-to-all-start.1 = ((bf16[3,576,2048]{2,0,1:T(4,128)(2,1)}), bf16[3,576,2048]{2,0,1:T(4,128)(2,1)}, u32[]{:S(2)}, u32[]{:S(2)}) async-start(bf16[3,576,2048]{2,0,1:T(4,128)(2,1)} %copy.145), calls=%async_computation.1 | async-start | bytes 18874368 | tf_op jit(solution)/shard_map/all_to_all | solution.py:161
  987.2 211.6 %all-to-all-start.3 = ((bf16[3,576,2048]{2,0,1:T(4,128)(2,1)}), bf16[3,576,2048]{2,0,1:T(4,128)(2,1)}, u32[]{:S(2)}, u32[]{:S(2)}) async-start(bf16[3,576,2048]{2,0,1:T(4,128)(2,1)} %copy.150), calls=%async_computation.3 | async-start | bytes 18874368 | tf_op jit(solution)/shard_map/all_to_all | solution.py:196
  992.5 321.7 %reduce-scatter.17.cloned.1.call-start = ((), (), s32[]{:S(2)}) async-start(), calls=%async_computation.16 | async-start | bytes 9437184 | tf_op jit(solution)/shard_map/reduce_scatter | solution.py:251
  1224.8 335.5 %reduce-scatter.13.cloned.1.call-start = ((), (), s32[]{:S(2)}) async-start(), calls=%async_computation.14 | async-start | bytes 28311552 | tf_op jit(solution)/shard_map/reduce_scatter | solution.py:248
  1293.7 402.5 %reduce-scatter.25.cloned.1.call-start = ((), (), s32[]{:S(2)}) async-start(), calls=%async_computation.20 | async-start | bytes 1081344
  1296.3 457.8 %reduce-scatter.27.cloned.1.call-start = ((), (), s32[]{:S(2)}) async-start(), calls=%async_computation.21 | async-start | bytes 589824
  1297.5 552.1 %reduce-scatter.23.cloned.1.call-start = ((), (), s32[]{:S(2)}) async-start(), calls=%async_computation.19 | async-start | bytes 15728640 | tf_op jit(solution)/shard_map/reduce_scatter | solution.py:272
  1314.1 566.1 %reduce-scatter.19.cloned.1.call-start = ((), (), s32[]{:S(2)}) async-start(), calls=%async_computation.17 | async-start | bytes 1310720 | tf_op jit(solution)/shard_map/reduce_scatter | solution.py:263
  1314.9 790.7 %reduce-scatter.21.cloned.1.call-start = ((), (), s32[]{:S(2)}) async-start(), calls=%async_computation.18 | async-start | bytes 31457280 | tf_op jit(solution)/shard_map/reduce_scatter | solution.py:269
  1341.8 218.5 %copy-start.53 = (u32[32]{0:T(128)S(1)}, u32[32]{0:T(128)}, u32[]{:S(2)}) copy-start(u32[32]{0:T(128)} %constant.82) | copy-start | bytes 388
  1341.8 355.8 %copy-start.9 = (bf16[192,2048]{1,0:T(8,128)(2,1)S(1)}, bf16[192,2048]{1,0:T(8,128)(2,1)}, u32[]{:S(2)}) copy-start(bf16[192,2048]{1,0:T(8,128)(2,1)} %param.13) | copy-start | bytes 2359300
  1341.8 810.5 %reduce-scatter.15.cloned.1.call-start = ((), (), s32[]{:S(2)}) async-start(), calls=%async_computation.15 | async-start | bytes 3932160 | tf_op jit(solution)/shard_map/reduce_scatter | solution.py:260
  (44 other events, 142.7 us)
Sparse Core Ops, SparseCore 0:
  11.0 159.8 all-gather.3
  174.0 75.5 all-gather.5
  1225.0 87.5 reduce-scatter.16
  1314.7 245.5 reduce-scatter.12
  1563.0 133.1 reduce-scatter.24
  1699.0 27.1 reduce-scatter.26
  1729.8 119.7 reduce-scatter.22
  1852.5 27.6 reduce-scatter.18
  1883.6 221.8 reduce-scatter.20
  2108.4 43.9 reduce-scatter.14
where the time goes:
time: 2170 us; the launch traced here: 2160 us
  waiting for transfers between devices  1260 us (58%)
  blocking collectives  451 us (21%)
  matrix products  198 us (9%)
  local copies, waits for them, and re-layouts  140 us (6%)
  other arithmetic  88.1 us (4%)
    reduce_scatter x1, waiting for transfers between devices, on_device(): lax.psum_scatter(grad_w_gate_up.astype(jnp.bfloat16), 'dp', scatter_dimen...  224 us
    reduce_scatter x1, waiting for transfers between devices, on_device(): lax.psum_scatter(grad_w_qkv.astype(jnp.bfloat16), 'expert', scatter_dimen...  218 us
    all_to_all x1, waiting for transfers between devices, on_device(): lax.all_to_all(expert_out, 'expert', split_axis=1, concat_axis=0, tiled=T...  206 us
    all_to_all x1, waiting for transfers between devices, on_device(): lax.all_to_all(grad_rows, 'expert', split_axis=1, concat_axis=0, tiled=True)  197 us
    all_to_all x1, blocking collectives, on_device(): lax.all_to_all(back_send, 'expert', split_axis=0, concat_axis=1, tiled=True)  160 us
    all_to_all x1, blocking collectives, on_device(): lax.all_to_all(send_rows, 'expert', split_axis=0, concat_axis=1, tiled=True)  159 us
    unnamed x12, waiting for transfers between devices  137 us
    unnamed x3, blocking collectives  90.6 us
  transfers between devices with their start and end apart: 12, of which 10 were waited for; matrix products, arithmetic and copies ran while one was open for 9% of the time, Pallas kernels for 0%

commit v1 on v0

--- a/solution.py
+++ b/solution.py
@@ -158,9 +158,11 @@
     expert_out = jnp.einsum(
         "erf,efd->erd", activated, w_down, preferred_element_type=jnp.float32
     ).astype(jnp.bfloat16)
-    returned = lax.all_to_all(
-        expert_out, "expert", split_axis=1, concat_axis=0, tiled=True
-    ).reshape(slot_count, model_dim)
+    see_the_modes = lambda array_in: jnp.concatenate(
+        lax.all_to_all(jnp.stack(jnp.split(array_in, lax.psum(1, "expert"), 1), 0), "expert", 0, 0),
+        0,
+    )
+    returned = see_the_modes(expert_out).reshape(slot_count, model_dim)
     picked = (
         jnp.take(returned, slot_flat, axis=0)
         .reshape(row_count, top_count, model_dim)

time: 2170 us -> 2080 us (0.959)
  waiting for transfers between devices: 1260 us -> 1210 us
  local copies, waits for them, and re-layouts: 140 us -> 113 us
    all_to_all x1, waiting for transfers between devices: 206 us -> 155 us  [on_device(): lax.all_to_all(jnp.stack(jnp.split(array_in, lax.psum(1, 'expert'), 1), 0...]
    convert_element_type x1 -> x0, local copies, waits for them, and re-layouts: 22.9 us -> none  [on_device(): expert_out = jnp.einsum('erf,efd->erd', activated, w_down, preferred_elem...]
where the time goes in v1:
time: 2080 us; the launch traced here: 2070 us
  waiting for transfers between devices  1210 us (58%)
  blocking collectives  451 us (22%)
  matrix products  198 us (10%)
  local copies, waits for them, and re-layouts  113 us (5%)
  other arithmetic  77.4 us (4%)
    reduce_scatter x1, waiting for transfers between devices, on_device(): lax.psum_scatter(grad_w_gate_up.astype(jnp.bfloat16), 'dp', scatter_dimen...  224 us
    reduce_scatter x1, waiting for transfers between devices, on_device(): lax.psum_scatter(grad_w_qkv.astype(jnp.bfloat16), 'expert', scatter_dimen...  219 us
    all_to_all x1, waiting for transfers between devices, on_device(): lax.all_to_all(grad_rows, 'expert', split_axis=1, concat_axis=0, tiled=True)  197 us
    all_to_all x1, blocking collectives, on_device(): lax.all_to_all(back_send, 'expert', split_axis=0, concat_axis=1, tiled=True)  160 us
    all_to_all x1, blocking collectives, on_device(): lax.all_to_all(send_rows, 'expert', split_axis=0, concat_axis=1, tiled=True)  159 us
    all_to_all x1, waiting for transfers between devices, on_device(): lax.all_to_all(jnp.stack(jnp.split(array_in, lax.psum(1, 'expert'), 1), 0...  155 us
    unnamed x12, waiting for transfers between devices  137 us
    unnamed x3, blocking collectives  90.6 us
  transfers between devices with their start and end apart: 12, of which 10 were waited for; matrix products, arithmetic and copies ran while one was open for 9% of the time, Pallas kernels for 0%

profile of v1, /device:TPU:0, one launch (start us, length us, event | category | flops | bytes accessed | tf_op | source)
XLA Modules:
  0.0 2071.3 jit_solution(16608478920202302566)
XLA Ops:
  12.1 43.5 %all-reduce.8 = (bf16[2048]{0:T(1024)(128)(2,1)S(1)}, bf16[2048]{0:T(1024)(128)(2,1)S(1)}, bf16[2048]{0:T(1024)(128)(2,1)S(1)}, bf16[2048]{0:T(1024)(128)(2,1)S(1)}) all-reduce(bf16[2048]{0:T(1024)(128)(2,1)S(1)} %dynamic-update-slice, bf16[2048]{0:T(1024)(128)(2,1)S(1)} %dynamic-update-slice.2, ...), channel_id=1, replica_groups=mesh['dp'=4,'expert'=8] {'dp','expert'}, use_global_device_ids=true, to_apply=%add | all-reduce | flops 8192 | bytes 32768
  55.6 41.7 %all-gather = bf16[32,64,24]{1,2,0:T(8,128)(2,1)S(1)} all-gather(bf16[1,64,24]{1,2,0:T(8,128)(2,1)} %bitcast.214), channel_id=1, replica_groups=mesh['dp'=4,'expert'=8] {'dp','expert'}, dimensions={0}, use_global_device_ids=true | all-gather | bytes 101376 | tf_op jit(solution)/shard_map/all_gather | solution.py:84
  101.9 69.1 %all-gather.4.cloned.1.call-done = bf16[2048,6144]{1,0:T(8,128)(2,1)} async-done(((bf16[64,6144]{1,0:T(8,128)(2,1)}), bf16[2048,6144]{1,0:T(8,128)(2,1)}) %all-gather.4.cloned.1.call-update) | async-done | bytes 25165840 | tf_op jit(solution)/shard_map/all_gather | solution.py:82
  191.6 57.9 %all-gather.6.cloned.1.call-done = bf16[2048,2048]{1,0:T(8,128)(2,1)} async-done(((bf16[64,2048]{1,0:T(8,128)(2,1)}), bf16[2048,2048]{1,0:T(8,128)(2,1)}) %all-gather.6.cloned.1.call-update) | async-done | bytes 8388624 | tf_op jit(solution)/shard_map/all_gather | solution.py:83
  265.6 159.0 %all_to_all.56 = bf16[24,72,2048]{2,1,0:T(8,128)(2,1)S(1)} all-to-all(bf16[24,72,2048]{2,1,0:T(8,128)(2,1)S(1)} %bitcast.191), channel_id=1, replica_groups=mesh['dp'=4,'expert'=8] {'expert'}, dimensions={0} | all-to-all | bytes 14155776 | tf_op jit(solution)/shard_map/all_to_all | solution.py:150
  428.2 24.3 %fusion.93 = f32[3,576,2048]{2,1,0:T(8,128)} fusion(bf16[3,576,2048]{2,1,0:T(8,128)(2,1)} %bitcast.188, bf16[3,2048,2048]{2,1,0:T(8,128)(2,1)} %param.24), kind=kOutput, calls=%fused_computation.188 | convolution fusion | flops 14495514624 | bytes 46399488 | tf_op jit(solution)/shard_map/erd,edf->erf/dot_general | solution.py:151
  486.3 155.1 %all-to-all-done.1 = bf16[8,3,72,2048]{3,2,1,0:T(8,128)(2,1)} async-done(((bf16[8,3,72,2048]{3,2,1,0:T(8,128)(2,1)}), bf16[8,3,72,2048]{3,2,1,0:T(8,128)(2,1)}, u32[]{:S(2)}, u32[]{:S(2)}) %all-to-all-start.1) | async-done | bytes 7077920 | tf_op jit(solution)/shard_map/all_to_all | solution.py:162
  641.5 16.6 gather_fusion
  663.3 14.1 scatter_custom_fusion
  677.4 159.9 %all_to_all.57 = bf16[24,72,2048]{2,1,0:T(8,128)(2,1)S(1)} all-to-all(bf16[24,72,2048]{2,1,0:T(8,128)(2,1)} %bitcast.194), channel_id=1, replica_groups=mesh['dp'=4,'expert'=8] {'expert'}, dimensions={0} | all-to-all | bytes 14155776 | tf_op jit(solution)/shard_map/all_to_all | solution.py:182
  841.0 22.3 %multiply_convert_fusion.1 = (bf16[3,576,1024]{2,1,0:T(8,128)(2,1)}, bf16[3,576,1024]{2,1,0:T(8,128)(2,1)}) fusion(f32[3,576,2048]{2,1,0:T(8,128)} %fusion.93, bf16[3,576,2048]{2,1,0:T(8,128)(2,1)} %bitcast.204, bf16[3,1024,2048]{2,1,0:T(8,128)(2,1)} %param.25), kind=kOutput, calls=%fused_computation.15 | convolution fusion | flops 7270760448 | bytes 40894464 | tf_op jit(solution)/shard_map/erd,efd->erf/dot_general | solution.py:183
  863.4 21.6 %convolution_convert_fusion.5 = bf16[3,576,2048]{2,1,0:T(8,128)(2,1)} fusion(bf16[3,2048,2048]{2,1,0:T(8,128)(2,1)} %param.24, bf16[3,576,1024]{2,1,0:T(8,128)(2,1)} %get-tuple-element.80, bf16[3,576,1024]{2,1,0:T(8,128)(2,1)} %get-tuple-element.79), kind=kOutput, calls=%fused_computation.24 | convolution fusion | flops 14513209344 | bytes 39321600 | tf_op jit(solution)/shard_map/erf,edf->erd/dot_general | solution.py:195
  910.8 197.3 %all-to-all-done.3 = bf16[3,576,2048]{2,0,1:T(4,128)(2,1)} async-done(((bf16[3,576,2048]{2,0,1:T(4,128)(2,1)}), bf16[3,576,2048]{2,0,1:T(4,128)(2,1)}, u32[]{:S(2)}, u32[]{:S(2)}) %all-to-all-start.3) | async-done | bytes 7077920 | tf_op jit(solution)/shard_map/all_to_all | solution.py:198
  1170.3 32.4 %copy.155 = bf16[2048,6144]{0,1:T(8,128)(2,1)} copy(bf16[2048,6144]{1,0:T(8,128)(2,1)} %convolution_convert_fusion) | data formatting | bytes 50331648 | tf_op jit(solution)/shard_map/convert_element_type | solution.py:251
  1206.6 16.6 convolution_convert_fusion.4
  1224.2 26.6 %convolution_convert_fusion.1 = bf16[3,2048,2048]{2,1,0:T(8,128)(2,1)} fusion(bf16[3,576,2048]{2,1,0:T(8,128)(2,1)} %bitcast.189, bf16[3,576,1024]{2,1,0:T(8,128)(2,1)} %get-tuple-element.80, bf16[3,576,1024]{2,1,0:T(8,128)(2,1)} %get-tuple-element.79), kind=kOutput, calls=%fused_computation.5 | convolution fusion | flops 14522253312 | bytes 39321600 | tf_op jit(solution)/shard_map/erd,erf->edf/dot_general | solution.py:192
  1250.9 218.6 %reduce-scatter.13.cloned.1.call-done = bf16[2048,3,256]{0,2,1:T(8,128)(2,1)} async-done(((bf16[2048,3,2048]{0,2,1:T(8,128)(2,1)}), bf16[2048,3,256]{0,2,1:T(8,128)(2,1)}) %reduce-scatter.13.cloned.1.call-update) | async-done | bytes 3145744 | tf_op jit(solution)/shard_map/reduce_scatter | solution.py:250
  1470.2 135.2 %reduce-scatter.25.cloned.1.call-done = f32[64,24]{1,0:T(8,128)} async-done(((f32[2048,24]{1,0:T(8,128)}), f32[64,24]{1,0:T(8,128)}) %reduce-scatter.25.cloned.1.call-update) | async-done | bytes 6160
  1606.8 14.8 fusion.20
  1621.7 37.2 %all-reduce.7 = (f32[2048]{0:T(1024)S(1)}, f32[2048]{0:T(1024)S(1)}) all-reduce(f32[2048]{0:T(1024)S(1)} %get-tuple-element.65, f32[2048]{0:T(1024)S(1)} %get-tuple-element.63), channel_id=7, replica_groups=mesh['dp'=4,'expert'=8] {'dp','expert'}, use_global_device_ids=true, to_apply=%region_28.29.clone | all-reduce | flops 4096 | bytes 32768
  1675.3 83.5 %reduce-scatter.23.cloned.1.call-done = bf16[3,256,2048]{2,1,0:T(8,128)(2,1)} async-done(((bf16[3,1024,2048]{2,1,0:T(8,128)(2,1)}), bf16[3,256,2048]{2,1,0:T(8,128)(2,1)}) %reduce-scatter.23.cloned.1.call-update) | async-done | bytes 3145744 | tf_op jit(solution)/shard_map/reduce_scatter | solution.py:274
  1764.2 25.2 %reduce-scatter.19.cloned.1.call-done = bf16[256,512]{1,0:T(8,128)(2,1)} async-done(((bf16[256,2048]{1,0:T(8,128)(2,1)}), bf16[256,512]{1,0:T(8,128)(2,1)}) %reduce-scatter.19.cloned.1.call-update) | async-done | bytes 262160 | tf_op jit(solution)/shard_map/reduce_scatter | solution.py:265
  1791.2 223.5 %reduce-scatter.21.cloned.1.call-done = bf16[3,512,2048]{2,1,0:T(8,128)(2,1)} async-done(((bf16[3,2048,2048]{2,1,0:T(8,128)(2,1)}), bf16[3,512,2048]{2,1,0:T(8,128)(2,1)}) %reduce-scatter.21.cloned.1.call-update) | async-done | bytes 6291472 | tf_op jit(solution)/shard_map/reduce_scatter | solution.py:271
  2023.8 37.7 %reduce-scatter.15.cloned.1.call-done = bf16[512,3,256]{0,2,1:T(8,128)(2,1)} async-done(((bf16[2048,3,256]{0,2,1:T(8,128)(2,1)}), bf16[512,3,256]{0,2,1:T(8,128)(2,1)}) %reduce-scatter.15.cloned.1.call-update) | async-done | bytes 786448 | tf_op jit(solution)/shard_map/reduce_scatter | solution.py:262
  (254 shorter events, 221.8 us)
Async XLA Ops:
  7.2 163.8 %copy-start.7 = (bf16[192,2048]{1,0:T(8,128)(2,1)S(1)}, bf16[192,2048]{1,0:T(8,128)(2,1)}, u32[]{:S(2)}) copy-start(bf16[192,2048]{1,0:T(8,128)(2,1)} %param.13) | copy-start | bytes 2359300
  7.2 163.8 %all-gather.4.cloned.1.call-start = ((), (), s32[]{:S(2)}) async-start(), calls=%async_computation.12 | async-start | bytes 25952256 | tf_op jit(solution)/shard_map/all_gather | solution.py:82
  7.9 241.6 %all-gather.6.cloned.1.call-start = ((), (), s32[]{:S(2)}) async-start(), calls=%async_computation.13 | async-start | bytes 8650752 | tf_op jit(solution)/shard_map/all_gather | solution.py:83
  55.6 126.5 %copy-start.30 = (f32[2048]{0:T(1024)}, f32[2048]{0:T(1024)S(1)}, u32[]{:S(2)}) copy-start(f32[2048]{0:T(1024)S(1)} %convert_element_type.154) | copy-start | bytes 24580
  55.6 126.8 %copy-start.34 = (f32[2048]{0:T(1024)}, f32[2048]{0:T(1024)S(1)}, u32[]{:S(2)}) copy-start(f32[2048]{0:T(1024)S(1)} %convert_element_type.158) | copy-start | bytes 24580
  55.6 126.8 %copy-start.36 = (f32[2048]{0:T(1024)}, f32[2048]{0:T(1024)S(1)}, u32[]{:S(2)}) copy-start(f32[2048]{0:T(1024)S(1)} %convert_element_type.157) | copy-start | bytes 24580
  55.6 199.3 %copy-start.38 = (f32[2048]{0:T(1024)}, f32[2048]{0:T(1024)S(1)}, u32[]{:S(2)}) copy-start(f32[2048]{0:T(1024)S(1)} %convert_element_type.164) | copy-start | bytes 24580
  97.6 158.6 %copy-start.27 = (bf16[2048,24]{0,1:T(8,128)(2,1)}, bf16[2048,24]{0,1:T(8,128)(2,1)S(1)}, u32[]{:S(2)}) copy-start(bf16[2048,24]{0,1:T(8,128)(2,1)S(1)} %reshape.540) | copy-start | bytes 294916
  99.8 82.3 %copy-start.44 = (f32[192]{0:T(256)}, f32[192]{0:T(256)S(1)}, u32[]{:S(2)}) copy-start(f32[192]{0:T(256)S(1)} %add_rsqrt_fusion.3) | copy-start | bytes 2308
  101.9 83.0 %copy-start.25 = (f32[192,64]{1,0:T(8,128)}, f32[192,64]{1,0:T(8,128)S(1)}, u32[]{:S(2)}) copy-start(f32[192,64]{1,0:T(8,128)S(1)} %get-tuple-element.107) | copy-start | bytes 147460
  191.6 63.3 %copy-start.19 = (bf16[1,192,16,128]{3,2,1,0:T(8,128)(2,1)}, bf16[1,192,16,128]{3,2,1,0:T(8,128)(2,1)S(1)}, u32[]{:S(2)}) copy-start(bf16[1,192,16,128]{3,2,1,0:T(8,128)(2,1)S(1)} %copy.133) | copy-start | bytes 2359300
  458.8 14.0 copy-start.21
  480.6 160.9 %all-to-all-start.1 = ((bf16[8,3,72,2048]{3,2,1,0:T(8,128)(2,1)}), bf16[8,3,72,2048]{3,2,1,0:T(8,128)(2,1)}, u32[]{:S(2)}, u32[]{:S(2)}) async-start(bf16[8,3,72,2048]{3,2,1,0:T(8,128)(2,1)} %fusion.38), calls=%async_computation.1 | async-start | bytes 14155776 | tf_op jit(solution)/shard_map/all_to_all | solution.py:162
  896.5 211.6 %all-to-all-start.3 = ((bf16[3,576,2048]{2,0,1:T(4,128)(2,1)}), bf16[3,576,2048]{2,0,1:T(4,128)(2,1)}, u32[]{:S(2)}, u32[]{:S(2)}) async-start(bf16[3,576,2048]{2,0,1:T(4,128)(2,1)} %copy.142), calls=%async_computation.3 | async-start | bytes 18874368 | tf_op jit(solution)/shard_map/all_to_all | solution.py:198
  901.8 321.4 %reduce-scatter.17.cloned.1.call-start = ((), (), s32[]{:S(2)}) async-start(), calls=%async_computation.16 | async-start | bytes 9437184 | tf_op jit(solution)/shard_map/reduce_scatter | solution.py:253
  1134.1 335.4 %reduce-scatter.13.cloned.1.call-start = ((), (), s32[]{:S(2)}) async-start(), calls=%async_computation.14 | async-start | bytes 28311552 | tf_op jit(solution)/shard_map/reduce_scatter | solution.py:250
  1202.7 402.7 %reduce-scatter.25.cloned.1.call-start = ((), (), s32[]{:S(2)}) async-start(), calls=%async_computation.20 | async-start | bytes 1081344
  1205.3 458.0 %reduce-scatter.27.cloned.1.call-start = ((), (), s32[]{:S(2)}) async-start(), calls=%async_computation.21 | async-start | bytes 589824
  1206.5 552.3 %reduce-scatter.23.cloned.1.call-start = ((), (), s32[]{:S(2)}) async-start(), calls=%async_computation.19 | async-start | bytes 15728640 | tf_op jit(solution)/shard_map/reduce_scatter | solution.py:274
  1223.1 566.2 %reduce-scatter.19.cloned.1.call-start = ((), (), s32[]{:S(2)}) async-start(), calls=%async_computation.17 | async-start | bytes 1310720 | tf_op jit(solution)/shard_map/reduce_scatter | solution.py:265
  1223.9 790.8 %reduce-scatter.21.cloned.1.call-start = ((), (), s32[]{:S(2)}) async-start(), calls=%async_computation.18 | async-start | bytes 31457280 | tf_op jit(solution)/shard_map/reduce_scatter | solution.py:271
  1250.9 218.7 %copy-start.52 = (u32[32]{0:T(128)S(1)}, u32[32]{0:T(128)}, u32[]{:S(2)}) copy-start(u32[32]{0:T(128)} %constant.82) | copy-start | bytes 388
  1250.9 355.9 %copy-start.9 = (bf16[192,2048]{1,0:T(8,128)(2,1)S(1)}, bf16[192,2048]{1,0:T(8,128)(2,1)}, u32[]{:S(2)}) copy-start(bf16[192,2048]{1,0:T(8,128)(2,1)} %param.13) | copy-start | bytes 2359300
  1250.9 810.6 %reduce-scatter.15.cloned.1.call-start = ((), (), s32[]{:S(2)}) async-start(), calls=%async_computation.15 | async-start | bytes 3932160 | tf_op jit(solution)/shard_map/reduce_scatter | solution.py:262
  (43 other events, 117.6 us)
Sparse Core Ops, SparseCore 0:
  11.0 159.8 all-gather.3
  173.9 75.5 all-gather.5
  1134.2 87.4 reduce-scatter.16
  1224.0 245.5 reduce-scatter.12
  1472.2 133.1 reduce-scatter.24
  1608.2 27.2 reduce-scatter.26
  1639.1 119.6 reduce-scatter.22
  1761.7 27.6 reduce-scatter.18
  1792.8 221.8 reduce-scatter.20
  2017.5 43.9 reduce-scatter.14
